TPU v7x, 512 devices: a whole 4x8x8 slice. The times are simulated.
512 devices in a mesh: row: 16 (over y, core), col: 8 (over z), fib: 4 (over x).
Axes of the slice: x: 4, y: 8, z: 8, core: 2. Of those that a mesh axis runs over, the one named last changes fastest.
Arguments:
- values: bfloat16 [768, 12, 128, 128], P(('row', 'col'), 'fib'), may hold values from -3 to 3
- columns: int32 [768, 12], P(('row', 'col')), may hold values from 0 to 767, as said below
- counts: int32 [768], P(('row', 'col')), may hold values from 6 to 12, as said below
Outputs:
- square: bfloat16 [768, 12, 128, 128], P(('row', 'col'), 'fib')
- traces: float32 [2], replicated
Inputs may be any that keep to these rules, and one draw needn't show every extreme that they name: Slot 0 of block row i holds i. Every slot s >= 1 of row i, used or not, holds (i + o) mod 768 with 1 <= |o| <= 6, and the columns of one row are distinct. Row i uses slots 0 to counts[i] - 1; later slots are ignored. Some row uses all 12 slots.
All inputs are finite; a program needn't handle non-finite values.
Results may differ from a plain program's by a relative error of at most 0.001.
Values may be sent and summed in bfloat16 or wider, within the bound.
A program may use at most 128 MiB of HBM per device.

v0:
```python
import jax
import jax.numpy as jnp
from jax import lax
from jax.sharding import PartitionSpec as P

BAND = 6


def padded(array, sides, width):
    for axis, dim in sides:
        size, length = (lax.axis_size(axis), array.shape[dim])
        up = [(i, (i + 1) % size) for i in range(size)]
        down = [(j, i) for i, j in up]
        last = lax.slice_in_dim(array, length - width, length, axis=dim)
        initial = lax.slice_in_dim(array, 0, width, axis=dim)
        before = lax.ppermute(last, axis, up)
        after = lax.ppermute(initial, axis, down)
        array = jnp.concatenate([before, array, after], axis=dim)
    return array


def band_product(
    left_tiles, left_keep, fetch_index, target_cols, target_keep, window, window_cols, window_counts
):
    picked = jnp.take(window, fetch_index, axis=0)
    picked_cols = jnp.take(window_cols, fetch_index, axis=0)
    picked_counts = jnp.take(window_counts, fetch_index, axis=0)
    alive_slots = lax.broadcasted_iota(jnp.int32, picked_cols.shape, 1) < picked_counts[:, None]
    matches = (picked_cols[:, None, :] == target_cols[None, :, None]) & alive_slots[:, None, :]
    matches = matches & left_keep[:, None, None] & target_keep[None, :, None]
    chosen = jnp.einsum(
        "ajs,asxy->ajxy", matches.astype(jnp.bfloat16), picked, preferred_element_type=jnp.float32
    ).astype(jnp.bfloat16)
    return jnp.einsum("axy,ajyz->jxz", left_tiles, chosen, preferred_element_type=jnp.float32)


def body(values, columns, counts):
    rows_here = values.shape[0]
    share_count = values.shape[1]
    slot_count = columns.shape[1]
    block_total = rows_here * lax.axis_size(("row", "col"))
    fib_index = lax.axis_index("fib")
    full_rows = lax.all_gather(values, "fib", axis=1, tiled=True)
    window, window_cols, window_counts = (
        padded(full_rows, ((("row", "col"), 0),), BAND),
        padded(columns, ((("row", "col"), 0),), BAND),
        padded(counts, ((("row", "col"), 0),), BAND),
    )
    local_rows = jnp.arange(rows_here, dtype=jnp.int32)
    row_ids = lax.axis_index(("row", "col")) * rows_here + local_rows
    fetch_all = (columns - row_ids[:, None] + BAND) % block_total + local_rows[:, None]
    slot_ids = jnp.arange(slot_count, dtype=jnp.int32)
    keep_mask = slot_ids[None, :] < counts[:, None]
    first_slot = fib_index * share_count

    def one_row(operands):
        left_tiles, left_keep, fetch_index, target_cols, target_keep = operands
        return band_product(
            left_tiles,
            left_keep,
            fetch_index,
            target_cols,
            target_keep,
            window,
            window_cols,
            window_counts,
        )

    left_fetch = lax.dynamic_slice_in_dim(fetch_all, first_slot, share_count, 1)
    left_keep = lax.dynamic_slice_in_dim(keep_mask, first_slot, share_count, 1)
    partial_value = lax.map(one_row, (values, left_keep, left_fetch, columns, keep_mask))
    regrouped = lax.all_to_all(partial_value[None], "fib", split_axis=2, concat_axis=0, tiled=True)
    product = jnp.sum(regrouped, axis=0)
    is_first = (fib_index == 0).astype(jnp.float32)
    trace_values = is_first * jnp.sum(
        jnp.diagonal(values[:, 0].astype(jnp.float32), axis1=1, axis2=2)
    )
    trace_square = is_first * jnp.sum(jnp.diagonal(product[:, 0], axis1=1, axis2=2))
    traces = lax.psum(jnp.stack([trace_values, trace_square]), ("row", "col", "fib"))
    return (product.astype(jnp.bfloat16), traces)


def solution(mesh):
    in_specs = (P(("row", "col"), "fib", None, None), P(("row", "col"), None), P(("row", "col")))
    out_specs = (P(("row", "col"), "fib", None, None), P())
    return jax.shard_map(body, mesh=mesh, in_specs=in_specs, out_specs=out_specs, check_vma=False)
```

profile of v0, /device:TPU:1, one launch (start us, length us, event | category | flops | bytes accessed | tf_op | source)
XLA Modules:
  0.0 354.2 jit_solution(3832877042432415155)
XLA Ops:
  7.9 45.8 %all-gather.2.cloned.1.call-done = bf16[6,12,128,128]{3,2,1,0:T(8,128)(2,1)} async-done(((bf16[6,3,128,128]{3,2,1,0:T(8,128)(2,1)}), bf16[6,12,128,128]{3,2,1,0:T(8,128)(2,1)}) %all-gather.2.cloned.1.call-update) | async-done | bytes 2359312 | tf_op jit(solution)/shard_map/all_gather | solution.py:43
  53.7 3.3 collective-permute-start.4
  57.0 5.0 %collective-permute-start.5 = (bf16[6,12,128,128]{3,2,1,0:T(8,128)(2,1)}, bf16[6,12,128,128]{3,2,1,0:T(8,128)(2,1)}, u32[]{:S(2)}, u32[]{:S(2)}) collective-permute-start(bf16[6,12,128,128]{3,2,1,0:T(8,128)(2,1)} %all-gather.2.cloned.1.call-done), channel_id=1, source_target_pairs={{4,0},{8,4},{12,8},{16,12},{20,16},{24,20},{28,24},{32,28},{36,32}... | collective-permute-start | bytes 7077896 | tf_op jit(solution)/shard_map/ppermute | solution.py:17
  61.9 1.9 collective-permute-start
  63.8 4.9 %collective-permute-start.1 = (s32[6,12]{1,0:T(8,128)}, s32[6,12]{1,0:T(8,128)S(1)}, u32[]{:S(2)}, u32[]{:S(2)}) collective-permute-start(s32[6,12]{1,0:T(8,128)} %param.6), channel_id=1, source_target_pairs={{4,0},{8,4},{12,8},{16,12},{20,16},{24,20},{28,24},{32,28},{36,32}... | collective-permute-start | bytes 872 | tf_op jit(solution)/shard_map/ppermute | solution.py:17
  68.7 1.9 collective-permute-start.2
  70.7 0.7 iota_compare_fusion.1
  71.5 0.8 fusion.18
  72.3 39.8 %collective-permute-done.2 = s32[6]{0:T(128)S(1)} collective-permute-done((s32[6]{0:T(128)}, s32[6]{0:T(128)S(1)}, u32[]{:S(2)}, u32[]{:S(2)}) %collective-permute-start.2) | collective-permute-done | bytes 56 | tf_op jit(solution)/shard_map/ppermute | solution.py:16
  112.2 2.9 collective-permute-start.3
  115.1 1.5 collective-permute-done.3
  116.6 0.7 pad_add_fusion.1
  117.3 0.7 pad_add_fusion
  118.1 5.9 %pad_maximum_fusion = bf16[18,12,128,128]{3,2,1,0:T(8,128)(2,1)} fusion(bf16[6,12,128,128]{3,2,1,0:T(8,128)(2,1)} %collective-permute-done.5, bf16[6,12,128,128]{3,2,1,0:T(8,128)(2,1)} %all-gather.2.cloned.1.call-done, bf16[6,12,128,128]{3,2,1,0:T(8,128)(2,1)S(1)} %collective-permute-done.4), kind=kLoop, calls=%fused_computation.37 | loop fusion | flops 7077888 | bytes 14155776 | tf_op jit(solution)/shard_map/concatenate | solution.py:18
  123.9 50.9 %while.10 = (s32[]{:T(128)}, f32[6,12,128,128]{2,3,0,1:T(8,128)}, s32[6,3]{1,0:T(8,128)S(1)}, s32[18,12]{1,0:T(8,128)S(1)}, s32[6,12]{1,0:T(8,128)}, /*index=5*/...) while((s32[]{:T(128)}, f32[6,12,128,128]{2,3,0,1:T(8,128)}, ...), condition=%wide.region_1.2_spmd, body=%wide.region_0.1_spmd.sunk | while | flops 166333216 | bytes 9541871 | solution.py:71
  124.6 3.8 %gather_fusion = bf16[3,12,128,128]{3,2,1,0:T(8,128)(2,1)S(1)} fusion(bf16[18,12,128,128]{3,2,1,0:T(8,128)(2,1)} %get-tuple-element.178, s32[1024]{0:T(1024)S(1)} %pad_clamp_fusion.2), kind=kCustom, calls=%fused_computation.2.clone.1 | custom fusion | bytes 2359308 | tf_op jit(solution)/shard_map/while/body/eval_jaxpr/jit(_take)/gather | solution.py:25
  129.3 0.7 fusion.31
  130.0 0.9 convolution_convert_fusion.2
  131.0 1.5 fusion.32
  133.1 3.8 %gather_fusion = bf16[3,12,128,128]{3,2,1,0:T(8,128)(2,1)S(1)} fusion(bf16[18,12,128,128]{3,2,1,0:T(8,128)(2,1)} %get-tuple-element.178, s32[1024]{0:T(1024)S(1)} %pad_clamp_fusion.2), kind=kCustom, calls=%fused_computation.2.clone.1 | custom fusion | bytes 2359308 | tf_op jit(solution)/shard_map/while/body/eval_jaxpr/jit(_take)/gather | solution.py:25
  137.8 0.7 fusion.31
  138.5 0.9 convolution_convert_fusion.2
  139.4 1.5 fusion.32
  141.6 3.8 %gather_fusion = bf16[3,12,128,128]{3,2,1,0:T(8,128)(2,1)S(1)} fusion(bf16[18,12,128,128]{3,2,1,0:T(8,128)(2,1)} %get-tuple-element.178, s32[1024]{0:T(1024)S(1)} %pad_clamp_fusion.2), kind=kCustom, calls=%fused_computation.2.clone.1 | custom fusion | bytes 2359308 | tf_op jit(solution)/shard_map/while/body/eval_jaxpr/jit(_take)/gather | solution.py:25
  146.3 0.7 fusion.31
  147.0 0.9 convolution_convert_fusion.2
  147.9 1.5 fusion.32
  150.1 3.8 %gather_fusion = bf16[3,12,128,128]{3,2,1,0:T(8,128)(2,1)S(1)} fusion(bf16[18,12,128,128]{3,2,1,0:T(8,128)(2,1)} %get-tuple-element.178, s32[1024]{0:T(1024)S(1)} %pad_clamp_fusion.2), kind=kCustom, calls=%fused_computation.2.clone.1 | custom fusion | bytes 2359308 | tf_op jit(solution)/shard_map/while/body/eval_jaxpr/jit(_take)/gather | solution.py:25
  154.8 0.7 fusion.31
  155.5 0.9 convolution_convert_fusion.2
  156.4 1.5 fusion.32
  158.5 3.8 %gather_fusion = bf16[3,12,128,128]{3,2,1,0:T(8,128)(2,1)S(1)} fusion(bf16[18,12,128,128]{3,2,1,0:T(8,128)(2,1)} %get-tuple-element.178, s32[1024]{0:T(1024)S(1)} %pad_clamp_fusion.2), kind=kCustom, calls=%fused_computation.2.clone.1 | custom fusion | bytes 2359308 | tf_op jit(solution)/shard_map/while/body/eval_jaxpr/jit(_take)/gather | solution.py:25
  163.2 0.7 fusion.31
  163.9 0.9 convolution_convert_fusion.2
  164.9 1.5 fusion.32
  167.0 3.8 %gather_fusion = bf16[3,12,128,128]{3,2,1,0:T(8,128)(2,1)S(1)} fusion(bf16[18,12,128,128]{3,2,1,0:T(8,128)(2,1)} %get-tuple-element.178, s32[1024]{0:T(1024)S(1)} %pad_clamp_fusion.2), kind=kCustom, calls=%fused_computation.2.clone.1 | custom fusion | bytes 2359308 | tf_op jit(solution)/shard_map/while/body/eval_jaxpr/jit(_take)/gather | solution.py:25
  172.4 0.9 convolution_convert_fusion.2
  173.3 1.5 fusion.32
  174.8 5.0 %all-to-all-start = ((f32[1,6,12,128,128]{3,4,1,0,2:T(8,128)}), f32[1,6,12,128,128]{3,4,1,0,2:T(8,128)}, u32[]{:S(2)}, u32[]{:S(2)}) async-start(f32[1,6,12,128,128]{3,4,1,0,2:T(8,128)} %bitcast.60), calls=%async_computation | async-start | bytes 9437184 | tf_op jit(solution)/shard_map/all_to_all | solution.py:72
  179.9 3.3 copy.13
  183.2 6.5 %bitcast_convert_fusion = f32[6,128,128]{0,2,1:T(8,128)} fusion(bf16[6,1,128,128]{0,3,2,1:T(8,128)(2,1)} %copy.13), kind=kLoop, calls=%fused_computation.38 | loop fusion | flops 98304 | bytes 589824 | tf_op jit(solution)/shard_map/convert_element_type | solution.py:76
  189.7 1.8 gather_fusion.3
  192.7 40.7 %all-to-all-done = f32[1,6,12,128,128]{3,4,1,0,2:T(8,128)} async-done(((f32[1,6,12,128,128]{3,4,1,0,2:T(8,128)}), f32[1,6,12,128,128]{3,4,1,0,2:T(8,128)}, u32[]{:S(2)}, u32[]{:S(2)}) %all-to-all-start) | async-done | bytes 4718624 | tf_op jit(solution)/shard_map/all_to_all | solution.py:72
  233.4 2.9 reduce_sum.27
  236.4 7.6 %copy.21 = f32[6,1,128,128]{0,3,2,1:T(8,128)} copy(f32[6,1,128,128]{2,3,1,0:T(8,128)S(1)} %copy.33) | data formatting | bytes 786432
  244.0 1.8 gather_fusion.4
  247.2 99.0 %psum.7 = f32[2]{0:T(128)} all-reduce(f32[2]{0:T(128)S(1)} %pad_maximum_fusion.1), channel_id=1, replica_groups=mesh['row'=16,'col'=8,'fib'=4] {'row','col','fib'}, use_global_device_ids=true, to_apply=%region_5.6 | all-reduce | flops 2 | bytes 16 | tf_op jit(solution)/shard_map/psum | solution.py:79
  346.3 1.1 copy.15
  (81 shorter events, 12.5 us)
Async XLA Ops:
  7.2 46.5 %all-gather.2.cloned.1.call-start = ((), (), s32[]{:S(2)}) async-start(), calls=%async_computation.1 | async-start | bytes 2949120 | tf_op jit(solution)/shard_map/all_gather | solution.py:43
  53.7 64.4 %collective-permute-start.4 = (bf16[6,12,128,128]{3,2,1,0:T(8,128)(2,1)}, bf16[6,12,128,128]{3,2,1,0:T(8,128)(2,1)S(1)}, u32[]{:S(2)}, u32[]{:S(2)}) collective-permute-start(bf16[6,12,128,128]{3,2,1,0:T(8,128)(2,1)} %all-gather.2.cloned.1.call-done), channel_id=1, source_target_pairs={{0,4},{4,8},{8,12},{12,16},{16,20},{20,24},{24,28},{28,32},{32,36}... | collective-permute-start | bytes 7077896 | tf_op jit(solution)/shard_map/ppermute | solution.py:16
  57.0 61.1 %collective-permute-start.5 = (bf16[6,12,128,128]{3,2,1,0:T(8,128)(2,1)}, bf16[6,12,128,128]{3,2,1,0:T(8,128)(2,1)}, u32[]{:S(2)}, u32[]{:S(2)}) collective-permute-start(bf16[6,12,128,128]{3,2,1,0:T(8,128)(2,1)} %all-gather.2.cloned.1.call-done), channel_id=1, source_target_pairs={{4,0},{8,4},{12,8},{16,12},{20,16},{24,20},{28,24},{32,28},{36,32}... | collective-permute-start | bytes 7077896 | tf_op jit(solution)/shard_map/ppermute | solution.py:17
  61.9 55.4 %collective-permute-start = (s32[6,12]{1,0:T(8,128)}, s32[6,12]{1,0:T(8,128)S(1)}, u32[]{:S(2)}, u32[]{:S(2)}) collective-permute-start(s32[6,12]{1,0:T(8,128)} %param.6), channel_id=1, source_target_pairs={{0,4},{4,8},{8,12},{12,16},{16,20},{20,24},{24,28},{28,32},{32,36}... | collective-permute-start | bytes 872 | tf_op jit(solution)/shard_map/ppermute | solution.py:16
  63.8 53.5 %collective-permute-start.1 = (s32[6,12]{1,0:T(8,128)}, s32[6,12]{1,0:T(8,128)S(1)}, u32[]{:S(2)}, u32[]{:S(2)}) collective-permute-start(s32[6,12]{1,0:T(8,128)} %param.6), channel_id=1, source_target_pairs={{4,0},{8,4},{12,8},{16,12},{20,16},{24,20},{28,24},{32,28},{36,32}... | collective-permute-start | bytes 872 | tf_op jit(solution)/shard_map/ppermute | solution.py:17
  68.7 43.5 %collective-permute-start.2 = (s32[6]{0:T(128)}, s32[6]{0:T(128)S(1)}, u32[]{:S(2)}, u32[]{:S(2)}) collective-permute-start(s32[6]{0:T(128)} %param.7), channel_id=1, source_target_pairs={{0,4},{4,8},{8,12},{12,16},{16,20},{20,24},{24,28},{28,32},{32,36}... | collective-permute-start | bytes 80 | tf_op jit(solution)/shard_map/ppermute | solution.py:16
  112.2 4.4 %collective-permute-start.3 = (s32[6]{0:T(128)}, s32[6]{0:T(128)S(1)}, u32[]{:S(2)}, u32[]{:S(2)}) collective-permute-start(s32[6]{0:T(128)} %param.7), channel_id=1, source_target_pairs={{4,0},{8,4},{12,8},{16,12},{20,16},{24,20},{28,24},{32,28},{36,32}... | collective-permute-start | bytes 80 | tf_op jit(solution)/shard_map/ppermute | solution.py:17
  118.0 5.9 %copy-start = (bf16[6,3,128,128]{3,2,1,0:T(8,128)(2,1)S(1)}, bf16[6,3,128,128]{3,2,1,0:T(8,128)(2,1)}, u32[]{:S(2)}) copy-start(bf16[6,3,128,128]{3,2,1,0:T(8,128)(2,1)} %param.5) | copy-start | bytes 1769476
  174.8 58.6 %all-to-all-start = ((f32[1,6,12,128,128]{3,4,1,0,2:T(8,128)}), f32[1,6,12,128,128]{3,4,1,0,2:T(8,128)}, u32[]{:S(2)}, u32[]{:S(2)}) async-start(f32[1,6,12,128,128]{3,4,1,0,2:T(8,128)} %bitcast.60), calls=%async_computation | async-start | bytes 9437184 | tf_op jit(solution)/shard_map/all_to_all | solution.py:72
Sparse Core Ops, SparseCore 0:
  10.1 43.5 all-gather.1
where the time goes:
time: 355 us; the launch traced here: 354 us
  waiting for transfers between devices  129 us (36%)
  blocking collectives  99 us (28%)
  local copies, waits for them, and re-layouts  50 us (14%)
  starting transfers between devices  24.9 us (7%)
  other arithmetic  21.6 us (6%)
  between operations  15.5 us (4%)
  matrix products  14.4 us (4%)
    psum x1, blocking collectives, body(): lax.psum(jnp.stack([trace_values, trace_square]), ('row', 'col', 'fib'))  99 us
    all_gather x1, waiting for transfers between devices, body(): full_rows = lax.all_gather(values, 'fib', axis=1, tiled=True)  45.8 us
    all_to_all x1, waiting for transfers between devices, body(): lax.all_to_all(partial_value[None], 'fib', split_axis=2, concat_axis=0, t...  40.7 us
    ppermute x3, waiting for transfers between devices, padded(): before = lax.ppermute(last, axis, up)  39.8 us
    gather x6, local copies, waits for them, and re-layouts, band_product(): picked = jnp.take(window, fetch_index, axis=0)  22.7 us
    ppermute x3, starting transfers between devices, padded(): after = lax.ppermute(initial, axis, down)  12.7 us
    dot_general x6, matrix products, band_product(): jnp.einsum('axy,ajyz->jxz', left_tiles, chosen, preferred_element_type=jn...  8.83 us
    unnamed x6, local copies, waits for them, and re-layouts  8.81 us
  transfers between devices with their start and end apart: 8, of which 4 were waited for; matrix products, arithmetic and copies ran while one was open for 4% of the time, Pallas kernels for 0%

commit v1 on v0

--- a/solution.py
+++ b/solution.py
@@ -40,7 +40,25 @@
     slot_count = columns.shape[1]
     block_total = rows_here * lax.axis_size(("row", "col"))
     fib_index = lax.axis_index("fib")
-    full_rows = lax.all_gather(values, "fib", axis=1, tiled=True)
+    length_2, index, width_2 = (lax.axis_size("fib"), lax.axis_index("fib"), values.shape[1])
+    ahead = [(i_2, (i_2 + 1) % length_2) for i_2 in range(length_2)]
+    left = [(i_2, (i_2 - 1) % length_2) for i_2 in range(length_2)]
+    full_rows = jnp.zeros(
+        (*values.shape[:1], length_2 * width_2, *values.shape[1 + 1 :]), values.dtype
+    )
+    full_rows = lax.dynamic_update_slice_in_dim(full_rows, values, index * width_2, axis=1)
+    from_left = from_right = values
+    half = length_2 // 2
+    for step in range(1, half + 1):
+        from_left = lax.ppermute(from_left, "fib", ahead)
+        full_rows = lax.dynamic_update_slice_in_dim(
+            full_rows, from_left, (index - step) % length_2 * width_2, axis=1
+        )
+        if step < length_2 - half:
+            from_right = lax.ppermute(from_right, "fib", left)
+            full_rows = lax.dynamic_update_slice_in_dim(
+                full_rows, from_right, (index + step) % length_2 * width_2, axis=1
+            )
     window, window_cols, window_counts = (
         padded(full_rows, ((("row", "col"), 0),), BAND),
         padded(columns, ((("row", "col"), 0),), BAND),

time: 355 us -> 328 us (0.924)
  waiting for transfers between devices: 129 us -> 101 us
  starting transfers between devices: 24.9 us -> 47.2 us
  between operations: 15.5 us -> 2.27 us
  blocking collectives: 99 us -> 94.9 us
    all_gather x1 -> x0, waiting for transfers between devices: 45.8 us -> none  [body(): full_rows = lax.all_gather(values, 'fib', axis=1, tiled=True)]
    ppermute x0 -> x3, waiting for transfers between devices: none -> 16.3 us  [the longest x2 16.3 us: body(): from_left = lax.ppermute(from_left, 'fib', ahead)]
    ppermute x0 -> x3, starting transfers between devices: none -> 13.9 us  [the longest x2 10.7 us: body(): from_left = lax.ppermute(from_left, 'fib', ahead)]
    ppermute x3, starting transfers between devices: 12.7 us -> 17.6 us  [padded(): after = lax.ppermute(initial, axis, down)]
    eq x6, local copies, waits for them, and re-layouts: 4.19 us -> 0.06 us  [band_product(): picked_cols[:, None, :] == target_cols[None, :, None]]
    psum x1, blocking collectives: 99 us -> 94.9 us  [body(): lax.psum(jnp.stack([trace_values, trace_square]), ('row', 'col', 'fib'))]
    unnamed x6 -> x10, local copies, waits for them, and re-layouts: 8.81 us -> 8.85 us
  transfers between devices with their start and end apart: 8 -> 10, of which waited for: 4 -> 5; matrix products, arithmetic and copies ran while one was open for 4% -> 4% of each run, Pallas kernels for 0% -> 0%
where the time goes in v1:
time: 328 us; the launch traced here: 327 us
  waiting for transfers between devices  101 us (31%)
  blocking collectives  94.9 us (29%)
  local copies, waits for them, and re-layouts  48.9 us (15%)
  starting transfers between devices  47.2 us (14%)
  other arithmetic  18.9 us (6%)
  matrix products  14.5 us (4%)
    psum x1, blocking collectives, body(): lax.psum(jnp.stack([trace_values, trace_square]), ('row', 'col', 'fib'))  94.9 us
    ppermute x3, waiting for transfers between devices, padded(): before = lax.ppermute(last, axis, up)  41 us
    all_to_all x1, waiting for transfers between devices, body(): lax.all_to_all(partial_value[None], 'fib', split_axis=2, concat_axis=0, t...  40.9 us
    gather x6, local copies, waits for them, and re-layouts, band_product(): picked = jnp.take(window, fetch_index, axis=0)  22.7 us
    ppermute x3, starting transfers between devices, padded(): after = lax.ppermute(initial, axis, down)  17.6 us
    ppermute x2, waiting for transfers between devices, body(): from_left = lax.ppermute(from_left, 'fib', ahead)  16.3 us
    ppermute x2, starting transfers between devices, body(): from_left = lax.ppermute(from_left, 'fib', ahead)  10.7 us
    ppermute x3, starting transfers between devices, padded(): before = lax.ppermute(last, axis, up)  10.6 us
  transfers between devices with their start and end apart: 10, of which 5 were waited for; matrix products, arithmetic and copies ran while one was open for 4% of the time, Pallas kernels for 0%

profile of v1, /device:TPU:1, one launch (start us, length us, event | category | flops | bytes accessed | tf_op | source)
XLA Modules:
  0.0 327.5 jit_solution(2972432660495729232)
XLA Ops:
  0.6 4.1 %collective-permute-start.4 = (bf16[6,3,128,128]{3,2,1,0:T(8,128)(2,1)}, bf16[6,3,128,128]{3,2,1,0:T(8,128)(2,1)S(1)}, u32[]{:S(2)}, u32[]{:S(2)}) collective-permute-start(bf16[6,3,128,128]{3,2,1,0:T(8,128)(2,1)} %param.5), channel_id=1, source_target_pairs={{0,1},{1,2},{2,3},{3,0},{4,5},{5,6},{6,7},{7,4},{8,9},{9,10},{10,1... | collective-permute-start | bytes 1769480 | tf_op jit(solution)/shard_map/ppermute | solution.py:53
  4.7 3.2 collective-permute-start.5
  7.9 5.5 %collective-permute-done.4 = bf16[6,3,128,128]{3,2,1,0:T(8,128)(2,1)S(1)} collective-permute-done((bf16[6,3,128,128]{3,2,1,0:T(8,128)(2,1)}, bf16[6,3,128,128]{3,2,1,0:T(8,128)(2,1)S(1)}, u32[]{:S(2)}, u32[]{:S(2)}) %collective-permute-start.4) | collective-permute-done | bytes 589856 | tf_op jit(solution)/shard_map/ppermute | solution.py:53
  13.5 6.7 %collective-permute-start.6 = (bf16[6,3,128,128]{3,2,1,0:T(8,128)(2,1)S(1)}, bf16[6,3,128,128]{3,2,1,0:T(8,128)(2,1)}, u32[]{:S(2)}, u32[]{:S(2)}) collective-permute-start(bf16[6,3,128,128]{3,2,1,0:T(8,128)(2,1)S(1)} %collective-permute-done.4), channel_id=1, source_target_pairs={{0,1},{1,2},{2,3},{3,0},{4,5},{5,6},{6,7},{7,4},{8,9},{9,10},{10,1... | collective-permute-start | bytes 1769480 | tf_op jit(solution)/shard_map/ppermute | solution.py:53
  21.0 1.2 constant_dynamic-update-slice_fusion.1
  22.2 10.8 %collective-permute-done.6 = bf16[6,3,128,128]{3,2,1,0:T(8,128)(2,1)} collective-permute-done((bf16[6,3,128,128]{3,2,1,0:T(8,128)(2,1)S(1)}, bf16[6,3,128,128]{3,2,1,0:T(8,128)(2,1)}, u32[]{:S(2)}, u32[]{:S(2)}) %collective-permute-start.6) | collective-permute-done | bytes 589856 | tf_op jit(solution)/shard_map/ppermute | solution.py:53
  32.9 1.1 constant_dynamic-update-slice_fusion
  34.1 6.7 %collective-permute-start.7 = (bf16[6,12,128,128]{3,2,1,0:T(8,128)(2,1)S(1)}, bf16[6,12,128,128]{3,2,1,0:T(8,128)(2,1)}, u32[]{:S(2)}, u32[]{:S(2)}) collective-permute-start(bf16[6,12,128,128]{3,2,1,0:T(8,128)(2,1)S(1)} %constant_dynamic-update-slice_fusion), channel_id=1, source_target_pairs={{0,4},{4,8},{8,12},{12,16},{16,20},{20,24},{24,28},{28,32},{32,36}... | collective-permute-start | bytes 7077896 | tf_op jit(solution)/shard_map/ppermute | solution.py:16
  40.8 10.9 %collective-permute-start.8 = (bf16[6,12,128,128]{3,2,1,0:T(8,128)(2,1)S(1)}, bf16[6,12,128,128]{3,2,1,0:T(8,128)(2,1)}, u32[]{:S(2)}, u32[]{:S(2)}) collective-permute-start(bf16[6,12,128,128]{3,2,1,0:T(8,128)(2,1)S(1)} %constant_dynamic-update-slice_fusion), channel_id=1, source_target_pairs={{4,0},{8,4},{12,8},{16,12},{20,16},{24,20},{28,24},{32,28},{36,32}... | collective-permute-start | bytes 7077896 | tf_op jit(solution)/shard_map/ppermute | solution.py:17
  51.7 1.9 collective-permute-start
  53.6 4.9 %collective-permute-start.1 = (s32[6,12]{1,0:T(8,128)S(1)}, s32[6,12]{1,0:T(8,128)S(1)}, u32[]{:S(2)}, u32[]{:S(2)}) collective-permute-start(s32[6,12]{1,0:T(8,128)S(1)} %copy-done.1), channel_id=1, source_target_pairs={{4,0},{8,4},{12,8},{16,12},{20,16},{24,20},{28,24},{32,28},{36,32}... | collective-permute-start | bytes 872 | tf_op jit(solution)/shard_map/ppermute | solution.py:17
  58.5 1.9 collective-permute-start.2
  60.8 41.0 %collective-permute-done.2 = s32[6]{0:T(128)S(1)} collective-permute-done((s32[6]{0:T(128)S(1)}, s32[6]{0:T(128)S(1)}, u32[]{:S(2)}, u32[]{:S(2)}) %collective-permute-start.2) | collective-permute-done | bytes 56 | tf_op jit(solution)/shard_map/ppermute | solution.py:16
  101.8 1.9 collective-permute-start.3
  103.7 2.4 collective-permute-done.3
  106.2 5.9 %pad_maximum_fusion = bf16[18,12,128,128]{3,2,1,0:T(8,128)(2,1)} fusion(bf16[6,12,128,128]{3,2,1,0:T(8,128)(2,1)} %collective-permute-done.8, bf16[6,12,128,128]{3,2,1,0:T(8,128)(2,1)S(1)} %constant_dynamic-update-slice_fusion, bf16[6,12,128,128]{3,2,1,0:T(8,128)(2,1)} %collective-permute-done.7), kind=kLoop, calls=%fused_computation.37 | loop fusion | flops 7077888 | bytes 14155776 | tf_op jit(solution)/shard_map/concatenate | solution.py:18
  112.1 46.9 %while.10 = (s32[]{:T(128)}, f32[6,12,128,128]{2,3,0,1:T(8,128)}, s32[6,3]{1,0:T(8,128)S(1)}, s32[18,12]{1,0:T(8,128)S(1)}, s32[6,12]{1,0:T(8,128)S(1)}, /*index...) while((s32[]{:T(128)}, f32[6,12,128,128]{2,3,0,1:T(8,128)}, ...), condition=%wide.region_1.2_spmd, body=%wide.region_0.1_spmd.sunk | while | flops 166333216 | bytes 9541871 | solution.py:89
  112.1 0.6 gather_fusion.1
  112.7 3.8 %gather_fusion = bf16[3,12,128,128]{3,2,1,0:T(8,128)(2,1)S(1)} fusion(bf16[18,12,128,128]{3,2,1,0:T(8,128)(2,1)} %get-tuple-element.178, s32[1024]{0:T(1024)S(1)} %pad_clamp_fusion.2), kind=kCustom, calls=%fused_computation.2.clone.1 | custom fusion | bytes 2359308 | tf_op jit(solution)/shard_map/while/body/eval_jaxpr/jit(_take)/gather | solution.py:25
  117.5 0.9 convolution_convert_fusion.2
  118.4 1.5 fusion.32
  120.6 3.8 %gather_fusion = bf16[3,12,128,128]{3,2,1,0:T(8,128)(2,1)S(1)} fusion(bf16[18,12,128,128]{3,2,1,0:T(8,128)(2,1)} %get-tuple-element.178, s32[1024]{0:T(1024)S(1)} %pad_clamp_fusion.2), kind=kCustom, calls=%fused_computation.2.clone.1 | custom fusion | bytes 2359308 | tf_op jit(solution)/shard_map/while/body/eval_jaxpr/jit(_take)/gather | solution.py:25
  125.3 0.9 convolution_convert_fusion.2
  126.2 1.5 fusion.32
  127.7 0.6 gather_fusion.1
  128.4 3.8 %gather_fusion = bf16[3,12,128,128]{3,2,1,0:T(8,128)(2,1)S(1)} fusion(bf16[18,12,128,128]{3,2,1,0:T(8,128)(2,1)} %get-tuple-element.178, s32[1024]{0:T(1024)S(1)} %pad_clamp_fusion.2), kind=kCustom, calls=%fused_computation.2.clone.1 | custom fusion | bytes 2359308 | tf_op jit(solution)/shard_map/while/body/eval_jaxpr/jit(_take)/gather | solution.py:25
  133.1 0.9 convolution_convert_fusion.2
  134.0 1.5 fusion.32
  135.5 0.6 gather_fusion.1
  136.2 3.8 %gather_fusion = bf16[3,12,128,128]{3,2,1,0:T(8,128)(2,1)S(1)} fusion(bf16[18,12,128,128]{3,2,1,0:T(8,128)(2,1)} %get-tuple-element.178, s32[1024]{0:T(1024)S(1)} %pad_clamp_fusion.2), kind=kCustom, calls=%fused_computation.2.clone.1 | custom fusion | bytes 2359308 | tf_op jit(solution)/shard_map/while/body/eval_jaxpr/jit(_take)/gather | solution.py:25
  140.9 0.9 convolution_convert_fusion.2
  141.8 1.5 fusion.32
  144.0 3.8 %gather_fusion = bf16[3,12,128,128]{3,2,1,0:T(8,128)(2,1)S(1)} fusion(bf16[18,12,128,128]{3,2,1,0:T(8,128)(2,1)} %get-tuple-element.178, s32[1024]{0:T(1024)S(1)} %pad_clamp_fusion.2), kind=kCustom, calls=%fused_computation.2.clone.1 | custom fusion | bytes 2359308 | tf_op jit(solution)/shard_map/while/body/eval_jaxpr/jit(_take)/gather | solution.py:25
  148.7 0.9 convolution_convert_fusion.2
  149.6 1.5 fusion.32
  151.8 3.8 %gather_fusion = bf16[3,12,128,128]{3,2,1,0:T(8,128)(2,1)S(1)} fusion(bf16[18,12,128,128]{3,2,1,0:T(8,128)(2,1)} %get-tuple-element.178, s32[1024]{0:T(1024)S(1)} %pad_clamp_fusion.2), kind=kCustom, calls=%fused_computation.2.clone.1 | custom fusion | bytes 2359308 | tf_op jit(solution)/shard_map/while/body/eval_jaxpr/jit(_take)/gather | solution.py:25
  156.5 0.9 convolution_convert_fusion.2
  157.4 1.5 fusion.32
  158.9 5.0 %all-to-all-start = ((f32[1,6,12,128,128]{3,4,1,0,2:T(8,128)}), f32[1,6,12,128,128]{3,4,1,0,2:T(8,128)}, u32[]{:S(2)}, u32[]{:S(2)}) async-start(f32[1,6,12,128,128]{3,4,1,0,2:T(8,128)} %bitcast.60), calls=%async_computation | async-start | bytes 9437184 | tf_op jit(solution)/shard_map/all_to_all | solution.py:90
  164.0 3.3 %copy.13 = bf16[6,1,128,128]{0,3,2,1:T(8,128)(2,1)} copy(bf16[6,1,128,128]{3,2,1,0:T(8,128)(2,1)S(1)} %slice.6) | data formatting | bytes 393216 | tf_op jit(solution)/shard_map/slice | solution.py:94
  167.3 6.5 %bitcast_convert_fusion = f32[6,128,128]{0,2,1:T(8,128)} fusion(bf16[6,1,128,128]{0,3,2,1:T(8,128)(2,1)} %copy.13), kind=kLoop, calls=%fused_computation.38 | loop fusion | flops 98304 | bytes 589824 | tf_op jit(solution)/shard_map/convert_element_type | solution.py:94
  173.8 1.8 gather_fusion.3
  176.8 40.9 %all-to-all-done = f32[1,6,12,128,128]{3,4,1,0,2:T(8,128)} async-done(((f32[1,6,12,128,128]{3,4,1,0,2:T(8,128)}), f32[1,6,12,128,128]{3,4,1,0,2:T(8,128)}, u32[]{:S(2)}, u32[]{:S(2)}) %all-to-all-start) | async-done | bytes 4718624 | tf_op jit(solution)/shard_map/all_to_all | solution.py:90
  217.7 2.9 reduce_sum.27
  220.6 7.6 %copy.21 = f32[6,1,128,128]{0,3,2,1:T(8,128)} copy(f32[6,1,128,128]{2,3,1,0:T(8,128)S(1)} %copy.33) | data formatting | bytes 786432
  228.3 1.8 gather_fusion.4
  231.5 94.9 %psum.7 = f32[2]{0:T(128)} all-reduce(f32[2]{0:T(128)S(1)} %pad_maximum_fusion.1), channel_id=1, replica_groups=mesh['row'=16,'col'=8,'fib'=4] {'row','col','fib'}, use_global_device_ids=true, to_apply=%region_5.6 | all-reduce | flops 2 | bytes 16 | tf_op jit(solution)/shard_map/psum | solution.py:97
  326.4 1.1 copy.15
  (93 shorter events, 10.2 us)
Async XLA Ops:
  0.6 20.1 %copy-start = (bf16[6,3,128,128]{3,2,1,0:T(8,128)(2,1)S(1)}, bf16[6,3,128,128]{3,2,1,0:T(8,128)(2,1)}, u32[]{:S(2)}) copy-start(bf16[6,3,128,128]{3,2,1,0:T(8,128)(2,1)} %param.5) | copy-start | bytes 1769476
  0.6 12.8 %collective-permute-start.4 = (bf16[6,3,128,128]{3,2,1,0:T(8,128)(2,1)}, bf16[6,3,128,128]{3,2,1,0:T(8,128)(2,1)S(1)}, u32[]{:S(2)}, u32[]{:S(2)}) collective-permute-start(bf16[6,3,128,128]{3,2,1,0:T(8,128)(2,1)} %param.5), channel_id=1, source_target_pairs={{0,1},{1,2},{2,3},{3,0},{4,5},{5,6},{6,7},{7,4},{8,9},{9,10},{10,1... | collective-permute-start | bytes 1769480 | tf_op jit(solution)/shard_map/ppermute | solution.py:53
  4.7 16.3 %collective-permute-start.5 = (bf16[6,3,128,128]{3,2,1,0:T(8,128)(2,1)}, bf16[6,3,128,128]{3,2,1,0:T(8,128)(2,1)}, u32[]{:S(2)}, u32[]{:S(2)}) collective-permute-start(bf16[6,3,128,128]{3,2,1,0:T(8,128)(2,1)} %param.5), channel_id=1, source_target_pairs={{0,3},{1,0},{2,1},{3,2},{4,7},{5,4},{6,5},{7,6},{8,11},{9,8},{10,9... | collective-permute-start | bytes 1769480 | tf_op jit(solution)/shard_map/ppermute | solution.py:58
  13.5 19.5 %collective-permute-start.6 = (bf16[6,3,128,128]{3,2,1,0:T(8,128)(2,1)S(1)}, bf16[6,3,128,128]{3,2,1,0:T(8,128)(2,1)}, u32[]{:S(2)}, u32[]{:S(2)}) collective-permute-start(bf16[6,3,128,128]{3,2,1,0:T(8,128)(2,1)S(1)} %collective-permute-done.4), channel_id=1, source_target_pairs={{0,1},{1,2},{2,3},{3,0},{4,5},{5,6},{6,7},{7,4},{8,9},{9,10},{10,1... | collective-permute-start | bytes 1769480 | tf_op jit(solution)/shard_map/ppermute | solution.py:53
  20.8 30.9 %copy-start.1 = (s32[6,12]{1,0:T(8,128)S(1)}, s32[6,12]{1,0:T(8,128)}, u32[]{:S(2)}) copy-start(s32[6,12]{1,0:T(8,128)} %param.6) | copy-start | bytes 868
  20.8 37.7 %copy-start.2 = (s32[6]{0:T(128)S(1)}, s32[6]{0:T(128)}, u32[]{:S(2)}) copy-start(s32[6]{0:T(128)} %param.7) | copy-start | bytes 76
  34.1 72.1 %collective-permute-start.7 = (bf16[6,12,128,128]{3,2,1,0:T(8,128)(2,1)S(1)}, bf16[6,12,128,128]{3,2,1,0:T(8,128)(2,1)}, u32[]{:S(2)}, u32[]{:S(2)}) collective-permute-start(bf16[6,12,128,128]{3,2,1,0:T(8,128)(2,1)S(1)} %constant_dynamic-update-slice_fusion), channel_id=1, source_target_pairs={{0,4},{4,8},{8,12},{12,16},{16,20},{20,24},{24,28},{28,32},{32,36}... | collective-permute-start | bytes 7077896 | tf_op jit(solution)/shard_map/ppermute | solution.py:16
  40.8 65.3 %collective-permute-start.8 = (bf16[6,12,128,128]{3,2,1,0:T(8,128)(2,1)S(1)}, bf16[6,12,128,128]{3,2,1,0:T(8,128)(2,1)}, u32[]{:S(2)}, u32[]{:S(2)}) collective-permute-start(bf16[6,12,128,128]{3,2,1,0:T(8,128)(2,1)S(1)} %constant_dynamic-update-slice_fusion), channel_id=1, source_target_pairs={{4,0},{8,4},{12,8},{16,12},{20,16},{24,20},{28,24},{32,28},{36,32}... | collective-permute-start | bytes 7077896 | tf_op jit(solution)/shard_map/ppermute | solution.py:17
  51.7 54.4 %collective-permute-start = (s32[6,12]{1,0:T(8,128)S(1)}, s32[6,12]{1,0:T(8,128)S(1)}, u32[]{:S(2)}, u32[]{:S(2)}) collective-permute-start(s32[6,12]{1,0:T(8,128)S(1)} %copy-done.1), channel_id=1, source_target_pairs={{0,4},{4,8},{8,12},{12,16},{16,20},{20,24},{24,28},{28,32},{32,36}... | collective-permute-start | bytes 872 | tf_op jit(solution)/shard_map/ppermute | solution.py:16
  53.6 52.5 %collective-permute-start.1 = (s32[6,12]{1,0:T(8,128)S(1)}, s32[6,12]{1,0:T(8,128)S(1)}, u32[]{:S(2)}, u32[]{:S(2)}) collective-permute-start(s32[6,12]{1,0:T(8,128)S(1)} %copy-done.1), channel_id=1, source_target_pairs={{4,0},{8,4},{12,8},{16,12},{20,16},{24,20},{28,24},{32,28},{36,32}... | collective-permute-start | bytes 872 | tf_op jit(solution)/shard_map/ppermute | solution.py:17
  58.5 43.2 %collective-permute-start.2 = (s32[6]{0:T(128)S(1)}, s32[6]{0:T(128)S(1)}, u32[]{:S(2)}, u32[]{:S(2)}) collective-permute-start(s32[6]{0:T(128)S(1)} %copy-done.2), channel_id=1, source_target_pairs={{0,4},{4,8},{8,12},{12,16},{16,20},{20,24},{24,28},{28,32},{32,36}... | collective-permute-start | bytes 80 | tf_op jit(solution)/shard_map/ppermute | solution.py:16
  101.8 4.3 %collective-permute-start.3 = (s32[6]{0:T(128)S(1)}, s32[6]{0:T(128)S(1)}, u32[]{:S(2)}, u32[]{:S(2)}) collective-permute-start(s32[6]{0:T(128)S(1)} %copy-done.2), channel_id=1, source_target_pairs={{4,0},{8,4},{12,8},{16,12},{20,16},{24,20},{28,24},{32,28},{36,32}... | collective-permute-start | bytes 80 | tf_op jit(solution)/shard_map/ppermute | solution.py:17
  158.9 58.8 %all-to-all-start = ((f32[1,6,12,128,128]{3,4,1,0,2:T(8,128)}), f32[1,6,12,128,128]{3,4,1,0,2:T(8,128)}, u32[]{:S(2)}, u32[]{:S(2)}) async-start(f32[1,6,12,128,128]{3,4,1,0,2:T(8,128)} %bitcast.60), calls=%async_computation | async-start | bytes 9437184 | tf_op jit(solution)/shard_map/all_to_all | solution.py:90
